TPU v7x, 32 devices: a whole 2x2x4 slice. The times are simulated.
32 devices in a mesh: energy: 16 (over z, y, x), slab: 2 (over core).
Axes of the slice: x: 2, y: 2, z: 4, core: 2. Of those that a mesh axis runs over, the one named last changes fastest.
Arguments:
- green_ret: bfloat16 [48, 4, 3, 2, 192, 192], P('energy', 'slab'), may hold values from -0.3125 to 0.3125
- sigma_less: bfloat16 [48, 4, 2, 192, 192], P('energy', 'slab'), may hold values from -6 to 6
- screened: float32 [48, 4, 2, 36864], P(None, 'slab', None, 'energy'), may hold values from -4 to 4
Outputs:
- sigma_new: bfloat16 [48, 4, 2, 192, 192], P('energy', 'slab')
- renewed: bfloat16 [48, 4, 2, 192, 192], P('energy', 'slab')
All inputs are finite; a program needn't handle non-finite values.
Results may differ from a plain program's by a relative error of at most 0.0085.
Values may be sent and summed in bfloat16 or wider, within the bound.
No kernel may reach another device: no remote copies, remote signals or barrier semaphores. Data moves between devices by JAX's collectives and lax.ppermute only.
A program may use at most 128 MiB of HBM per device.

v0:
```python
import math

import jax
import jax.numpy as jnp
from jax import lax
from jax.sharding import PartitionSpec as P


def with_halo(cells, sides, width):
    for axis, dim in sides:
        count = lax.axis_size(axis)
        ends = count - 1
        head = lax.slice_in_dim(cells, 0, width, axis=dim)
        tail = lax.slice_in_dim(cells, cells.shape[dim] - width, cells.shape[dim], axis=dim)
        cells = jnp.concatenate(
            [
                lax.ppermute(tail, axis, [(i, (i + 1) % count) for i in range(ends)]),
                cells,
                lax.ppermute(head, axis, [((i + 1) % count, i) for i in range(ends)]),
            ],
            axis=dim,
        )
    return cells


def cmul_adj(left, right):
    lr = left[..., 0, :, :]
    li = left[..., 1, :, :]
    rr = right[..., 0, :, :]
    ri = right[..., 1, :, :]
    real = jnp.einsum(
        "...ab,...cb->...ac", lr, rr, preferred_element_type=jnp.float32
    ) + jnp.einsum("...ab,...cb->...ac", li, ri, preferred_element_type=jnp.float32)
    imag = jnp.einsum(
        "...ab,...cb->...ac", li, rr, preferred_element_type=jnp.float32
    ) - jnp.einsum("...ab,...cb->...ac", lr, ri, preferred_element_type=jnp.float32)
    return jnp.stack([real, imag], axis=-3)


def cmul_plain(left, right):
    lr = left[..., 0, :, :]
    li = left[..., 1, :, :]
    rr = right[..., 0, :, :]
    ri = right[..., 1, :, :]
    real = jnp.einsum(
        "...ab,...bc->...ac", lr, rr, preferred_element_type=jnp.float32
    ) - jnp.einsum("...ab,...bc->...ac", li, ri, preferred_element_type=jnp.float32)
    imag = jnp.einsum(
        "...ab,...bc->...ac", lr, ri, preferred_element_type=jnp.float32
    ) + jnp.einsum("...ab,...bc->...ac", li, rr, preferred_element_type=jnp.float32)
    return jnp.stack([real, imag], axis=-3)


def convolve(owned, interaction):
    energies = owned.shape[0]
    index = jnp.arange(energies, dtype=jnp.int32)
    phase = index[:, None] * index[None, :] % energies
    angle = phase.astype(jnp.float32) * (2.0 * math.pi / energies)
    cosine = jnp.cos(angle)
    sine = jnp.sin(angle)
    forward = jnp.stack(
        [jnp.stack([cosine, sine], axis=1), jnp.stack([-sine, cosine], axis=1)], axis=0
    )
    backward = jnp.stack(
        [jnp.stack([cosine, -sine], axis=1), jnp.stack([sine, cosine], axis=1)], axis=0
    )
    ghat = jnp.einsum(
        "pfqe,esqn->pfsn", forward, owned.astype(jnp.float32), precision=lax.Precision.HIGH
    )
    what = jnp.einsum("pfqe,esqn->pfsn", forward, interaction, precision=lax.Precision.HIGH)
    prod_real = ghat[0] * what[0] - ghat[1] * what[1]
    prod_imag = ghat[0] * what[1] + ghat[1] * what[0]
    product = jnp.stack([prod_real, prod_imag], axis=0)
    result = jnp.einsum("pfqe,qesn->fspn", backward, product, precision=lax.Precision.HIGH)
    result = result * (1.0 / (energies * math.sqrt(energies)))
    return result.astype(jnp.bfloat16)


def shards(green_ret, sigma_less, screened):
    energy_dev = sigma_less.shape[0]
    slab_dev = sigma_less.shape[1]
    order = sigma_less.shape[-1]
    padded = with_halo(sigma_less, (("slab", 1),), 1)
    total = None
    for k in range(3):
        coupling = green_ret[:, :, k]
        inner = cmul_adj(padded[:, k : k + slab_dev], coupling).astype(jnp.bfloat16)
        term = cmul_plain(coupling, inner)
        total = term if total is None else total + term
    lesser = total.astype(jnp.bfloat16).reshape(energy_dev, slab_dev, 2, order * order)
    owned = lax.all_to_all(lesser, "energy", split_axis=3, concat_axis=0, tiled=True)
    fresh = convolve(owned, screened)
    sigma_new = lax.all_to_all(fresh, "energy", split_axis=0, concat_axis=3, tiled=True)
    sigma_new = sigma_new.reshape(energy_dev, slab_dev, 2, order, order)
    diag = green_ret[:, :, 1]
    inner = cmul_adj(sigma_new, diag).astype(jnp.bfloat16)
    renewed = cmul_plain(diag, inner).astype(jnp.bfloat16)
    return (sigma_new, renewed)


def solution(mesh):
    in_specs = (
        P("energy", "slab", None, None, None, None),
        P("energy", "slab", None, None, None),
        P(None, "slab", None, "energy"),
    )
    out_specs = (P("energy", "slab", None, None, None), P("energy", "slab", None, None, None))
    return jax.shard_map(shards, mesh=mesh, in_specs=in_specs, out_specs=out_specs, check_vma=False)
```

profile of v0, /device:TPU:0, one launch (start us, length us, event | category | flops | bytes accessed | tf_op | source)
XLA Modules:
  0.0 409.0 jit_solution(5809366205787892165)
XLA Ops:
  0.6 2.4 fusion.62
  3.0 3.2 collective-permute-start
  6.2 1.3 collective-permute-start.1
  7.5 3.3 fusion.61
  11.0 1.1 copy-done
  12.8 0.3 fusion.16
  13.1 0.4 fusion.43
  13.9 1.4 fusion.11
  15.3 1.4 fusion.42
  16.7 2.8 copy.130
  19.5 3.1 stack.114
  22.6 2.7 fusion.10
  25.3 1.7 copy.133
  27.0 1.8 stack.115
  28.8 1.3 copy.213
  30.2 1.2 constant_dynamic-update-slice_fusion.1
  31.9 0.4 fusion.29
  32.2 0.4 fusion.28
  32.6 1.1 constant_dynamic-update-slice_fusion.2
  33.7 1.6 fusion.33
  35.3 1.4 fusion.32
  36.7 0.4 fusion.14
  37.0 0.4 fusion.37
  37.4 0.5 copy-done.3
  38.3 1.4 fusion.36
  39.7 1.4 fusion.13
  41.1 2.7 copy.121
  43.9 3.1 stack.111
  46.9 2.9 fusion.12
  49.8 1.7 copy.124
  51.5 1.8 stack.112
  53.4 1.8 fusion.18
  55.2 0.4 fusion.39
  55.6 0.9 copy-done.4
  56.4 1.6 fusion.19
  58.0 1.4 fusion.38
  59.5 1.4 fusion.9
  60.9 2.8 copy.139
  63.6 3.1 stack.117
  66.7 2.7 fusion.8
  69.4 1.7 copy.142
  71.1 1.8 stack.118
  72.9 3.4 fusion.4
  76.4 66.1 %copy.143 = bf16[3,2,2,36864]{0,2,1,3:T(2,128)(2,1)} copy(bf16[3,2,2,36864]{3,1,0,2:T(2,128)(2,1)S(1)} %fusion.4) | data formatting | bytes 1769472 | tf_op jit(solution)/shard_map/convert_element_type | solution.py:90
  142.5 56.9 %reshape.98 = bf16[16,2,13824]{2,1,0:T(2,128)(2,1)} reshape(bf16[36864,2,2,3]{3,2,1,0:T(2,128)(2,1)} %bitcast.187) | data formatting | bytes 1769472
  199.4 7.7 %all-to-all-start = ((bf16[16,2,13824]{2,1,0:T(2,128)(2,1)}), bf16[16,2,13824]{2,1,0:T(2,128)(2,1)}, u32[]{:S(2)}, u32[]{:S(2)}) async-start(bf16[16,2,13824]{2,1,0:T(2,128)(2,1)} %reshape.98), calls=%async_computation | async-start | bytes 1769472 | tf_op jit(solution)/shard_map/all_to_all | solution.py:91
  207.4 2.5 convolution_bitcast_fusion.1
  209.9 17.5 %all-to-all-done = bf16[16,2,13824]{2,1,0:T(2,128)(2,1)} async-done(((bf16[16,2,13824]{2,1,0:T(2,128)(2,1)}), bf16[16,2,13824]{2,1,0:T(2,128)(2,1)}, u32[]{:S(2)}, u32[]{:S(2)}) %all-to-all-start) | async-done | bytes 884768 | tf_op jit(solution)/shard_map/all_to_all | solution.py:91
  227.4 85.2 %reshape.99 = bf16[36864,2,2,3]{3,2,1,0:T(2,128)(2,1)} reshape(bf16[16,2,13824]{2,1,0:T(2,128)(2,1)} %all-to-all-done) | data formatting | bytes 1769472
  312.6 53.2 %copy.178 = bf16[3,2,2,16,2304]{4,3,2,1,0:T(8,128)(2,1)} copy(bf16[3,2,2,16,2304]{0,2,1,4,3:T(2,128)(2,1)} %bitcast.188) | data formatting | bytes 1769472 | tf_op jit(solution)/shard_map/all_to_all | solution.py:91
  365.8 1.8 copy.145
  367.6 0.7 convolution_bitcast_fusion.2
  368.6 0.9 fusion.2
  369.6 0.7 copy.149
  370.2 31.4 %all_to_all.33 = bf16[48,2,2,2304]{3,2,1,0:T(2,128)(2,1)S(1)} all-to-all(bf16[48,2,2,2304]{3,2,1,0:T(2,128)(2,1)S(1)} %copy.149), channel_id=1, replica_groups=mesh['energy'=16,'slab'=2] {'energy'}, dimensions={0} | all-to-all | bytes 1769472 | tf_op jit(solution)/shard_map/all_to_all | solution.py:93
  401.8 1.4 reshape.89
  403.9 1.1 copy.155
  404.9 0.4 fusion.20
  405.3 0.4 fusion.41
  405.7 0.4 fusion.21
  406.1 0.4 fusion.40
  406.5 0.4 fusion.25
  406.9 0.4 fusion.24
  407.5 1.5 copy.156
  (25 shorter events, 3.6 us)
Async XLA Ops:
  3.0 27.2 %collective-permute-start = (bf16[3,1,2,192,192]{4,3,1,0,2:T(8,128)(2,1)}, bf16[3,1,2,192,192]{4,3,1,0,2:T(8,128)(2,1)}, u32[]{:S(2)}, u32[]{:S(2)}) collective-permute-start(bf16[3,1,2,192,192]{4,3,1,0,2:T(8,128)(2,1)} %get-tuple-element.16), channel_id=1, source_target_pairs={{0,1},{2,3},{4,5},{6,7},{8,9},{10,11},{12,13},{14,15},{16,17},{18,... | collective-permute-start | bytes 1327112 | tf_op jit(solution)/shard_map/ppermute | solution.py:17
  6.2 26.4 %collective-permute-start.1 = (bf16[3,1,2,192,192]{4,3,1,0,2:T(8,128)(2,1)}, bf16[3,1,2,192,192]{4,3,1,0,2:T(8,128)(2,1)}, u32[]{:S(2)}, u32[]{:S(2)}) collective-permute-start(bf16[3,1,2,192,192]{4,3,1,0,2:T(8,128)(2,1)} %get-tuple-element.15), channel_id=1, source_target_pairs={{1,0},{3,2},{5,4},{7,6},{9,8},{11,10},{13,12},{15,14},{17,16},{19,... | collective-permute-start | bytes 1327112 | tf_op jit(solution)/shard_map/ppermute | solution.py:19
  10.8 1.3 copy-start
  30.2 1.5 copy-start.1
  33.7 1.6 copy-start.2
  37.0 0.9 copy-start.3
  55.2 1.3 copy-start.4
  71.1 1.8 copy-start.5
  199.4 28.1 %all-to-all-start = ((bf16[16,2,13824]{2,1,0:T(2,128)(2,1)}), bf16[16,2,13824]{2,1,0:T(2,128)(2,1)}, u32[]{:S(2)}, u32[]{:S(2)}) async-start(bf16[16,2,13824]{2,1,0:T(2,128)(2,1)} %reshape.98), calls=%async_computation | async-start | bytes 1769472 | tf_op jit(solution)/shard_map/all_to_all | solution.py:91
where the time goes:
time: 411 us; the launch traced here: 409 us
  local copies, waits for them, and re-layouts  308 us (75%)
  matrix products  34.3 us (8%)
  blocking collectives  31.4 us (8%)
  waiting for transfers between devices  17.5 us (4%)
  starting transfers between devices  12.2 us (3%)
  other arithmetic  4.19 us (1%)
    unnamed x19, local copies, waits for them, and re-layouts  150 us
    convert_element_type x1, local copies, waits for them, and re-layouts, shards(): total.astype(jnp.bfloat16).reshape(energy_dev, slab_dev, 2, order * order)  66.1 us
    all_to_all x2, local copies, waits for them, and re-layouts, shards(): lax.all_to_all(lesser, 'energy', split_axis=3, concat_axis=0, tiled=True)  55 us
    all_to_all x1, blocking collectives, shards(): lax.all_to_all(fresh, 'energy', split_axis=0, concat_axis=3, tiled=True)  31.4 us
    all_to_all x1, waiting for transfers between devices, shards(): lax.all_to_all(lesser, 'energy', split_axis=3, concat_axis=0, tiled=True)  17.5 us
    another operation x6, local copies, waits for them, and re-layouts, cmul_plain(): return jnp.stack([real, imag], axis=-3)  14.7 us
    dot_general x4, matrix products, cmul_plain(): jnp.einsum('...ab,...bc->...ac', li, rr, preferred_element_type=jnp.float32)  8.66 us
    sub x3, local copies, waits for them, and re-layouts, cmul_plain(): jnp.einsum('...ab,...bc->...ac', lr, rr, preferred_element_type=jnp.float32)  8.25 us
  transfers between devices with their start and end apart: 3, of which 1 were waited for; matrix products, arithmetic and copies ran while one was open for 6% of the time, Pallas kernels for 0%

commit v1 on v0

--- a/solution.py
+++ b/solution.py
@@ -1,9 +1,204 @@
+import functools
 import math
 
 import jax
 import jax.numpy as jnp
+import ml_dtypes
+import numpy as np
 from jax import lax
+from jax.experimental import pallas as pl
+from jax.experimental.pallas import tpu as pltpu
 from jax.sharding import PartitionSpec as P
+
+LANES = 128
+NT = (((1,), (1,)), ((), ()))
+NN = (((1,), (0,)), ((), ()))
+
+
+def dot(left, right, dims):
+    return lax.dot_general(left, right, dims, preferred_element_type=jnp.float32)
+
+
+def congruence(green, sigma):
+    order = green.shape[-1]
+    both = sigma.reshape(2 * order, order)
+    by_real = dot(both, green[0], NT)
+    by_imag = dot(both, green[1], NT)
+    inner_real = (by_real[:order] + by_imag[order:]).astype(jnp.bfloat16)
+    inner_imag = (by_real[order:] - by_imag[:order]).astype(jnp.bfloat16)
+    stacked = green.reshape(2 * order, order)
+    on_real = dot(stacked, inner_real, NN)
+    on_imag = dot(stacked, inner_imag, NN)
+    return on_real[:order] - on_imag[order:], on_imag[:order] + on_real[order:]
+
+
+def lesser_kernel(green_ref, sigma_ref, halo_ref, out_ref, stage):
+    order = green_ref.shape[-1]
+    rest = order - LANES
+    first = lax.axis_index("slab") == 0
+    halo_slab = jnp.where(first, 1, 0)
+    halo_block = jnp.where(first, 2, 0)
+    far = congruence(green_ref[0, halo_slab, halo_block], halo_ref[0, 0])
+    totals = []
+    for slab in range(2):
+        keep = halo_slab == slab
+        total = [jnp.where(keep, part, 0.0) for part in far]
+        for source in range(2):
+            term = congruence(green_ref[0, slab, source - slab + 1], sigma_ref[0, source])
+            total = [sum_ + new for sum_, new in zip(total, term)]
+        totals.append(total)
+    for part in range(2):
+        one, two = totals[0][part], totals[1][part]
+        rows = pl.ds(part, order, stride=2)
+        stage[0, rows, :] = one[:, :LANES]
+        stage[1, rows, :] = two[:, :LANES]
+        stage[2, rows, :] = jnp.concatenate([one[:, LANES:], two[:, LANES:]], axis=1)
+    devices, blocks, depth, _ = out_ref.shape
+    for block in range(blocks):
+        out_ref[:, block] = stage[block].reshape(devices, depth, LANES).astype(jnp.bfloat16)
+
+
+def convolve_kernel(got_ref, what_ref, fwd_ref, bwd_ref, out_ref, stage, packed):
+    devices, _, rows, _ = got_ref.shape
+    half = packed.shape[0] // 2
+    local = half // devices
+    depth = rows // local
+    owned = depth // 2
+    stage[...] = got_ref[:, 0].astype(jnp.float32).reshape(devices * rows, LANES)
+    for row in range(owned):
+        for part in range(2):
+            for energy in range(local):
+                picked = stage[pl.ds(energy * depth + row * 2 + part, devices, stride=rows), :]
+                at = part * half + energy * devices
+                packed[at : at + devices, row * LANES : (row + 1) * LANES] = picked.astype(jnp.bfloat16)
+    held = packed[...]
+    ghat = dot(fwd_ref[0], held, NN) + dot(fwd_ref[1], held, NN)
+    what = what_ref[0]
+    real = ghat[:half] * what[:half] - ghat[half:] * what[half:]
+    imag = ghat[:half] * what[half:] + ghat[half:] * what[:half]
+    product = jnp.concatenate([real, imag], axis=0)
+    high = product.astype(jnp.bfloat16)
+    low = (product - high.astype(jnp.float32)).astype(jnp.bfloat16)
+    result = dot(bwd_ref[0], high, NN) + dot(bwd_ref[1], high, NN) + dot(bwd_ref[0], low, NN)
+    for row in range(owned):
+        for part in range(2):
+            for energy in range(local):
+                at = part * half + energy * devices
+                stage[pl.ds(energy * depth + row * 2 + part, devices, stride=rows), :] = result[
+                    at : at + devices, row * LANES : (row + 1) * LANES
+                ]
+    out_ref[:, 0] = stage[...].reshape(devices, rows, LANES).astype(jnp.bfloat16)
+
+
+def renew_kernel(got_ref, green_ref, sigma_ref, renewed_ref, stage):
+    order = green_ref.shape[-1]
+    rest = order - LANES
+    for block in range(3):
+        stage[block] = got_ref[:, block].astype(jnp.float32).reshape(2 * order, LANES)
+    for part in range(2):
+        rows = pl.ds(part, order, stride=2)
+        one = stage[0, rows, :].astype(jnp.bfloat16)
+        two = stage[1, rows, :].astype(jnp.bfloat16)
+        mixed = stage[2, rows, :]
+        sigma_ref[0, 0, part, :, :LANES] = one
+        sigma_ref[0, 1, part, :, :LANES] = two
+        sigma_ref[0, 0, part, :, LANES:] = mixed[:, :rest].astype(jnp.bfloat16)
+        sigma_ref[0, 1, part, :, LANES:] = pltpu.roll(mixed, rest, 1)[:, :rest].astype(jnp.bfloat16)
+    for slab in range(2):
+        real, imag = congruence(green_ref[0, slab, 0], sigma_ref[0, slab])
+        renewed_ref[0, slab, 0] = real.astype(jnp.bfloat16)
+        renewed_ref[0, slab, 1] = imag.astype(jnp.bfloat16)
+
+
+def split_high_low(matrix):
+    high = matrix.astype(ml_dtypes.bfloat16)
+    low = (matrix - high.astype(np.float64)).astype(ml_dtypes.bfloat16)
+    return jnp.asarray(np.stack([high, low]))
+
+
+def transforms(energies, devices):
+    local = energies // devices
+    index = np.arange(energies)
+    angle = (index[:, None] * index[None, :] % energies) * (2.0 * math.pi / energies)
+    cosine, sine = np.cos(angle), np.sin(angle)
+    order = (np.arange(devices)[None, :] * local + np.arange(local)[:, None]).reshape(-1)
+    scale = 1.0 / (energies * math.sqrt(energies))
+    forward = np.block([[cosine[:, order], sine[:, order]], [-sine[:, order], cosine[:, order]]])
+    backward = scale * np.block([[cosine[order], -sine[order]], [sine[order], cosine[order]]])
+    plain = np.stack([np.stack([cosine, sine], 1), np.stack([-sine, cosine], 1)])
+    return split_high_low(forward), split_high_low(backward), jnp.asarray(plain, jnp.float32)
+
+
+def fast_shards(green_ret, sigma_less, screened):
+    devices = lax.axis_size("energy")
+    local, slabs, _, order, _ = sigma_less.shape
+    energies = local * devices
+    owned = order // devices
+    depth = 2 * owned
+    rows = depth * local
+    rest = order - LANES
+
+    edge = 1 - lax.axis_index("slab")
+    halo = lax.ppermute(
+        lax.dynamic_slice_in_dim(sigma_less, edge, 1, axis=1), "slab", [(0, 1), (1, 0)]
+    )
+    zeros = (0,) * 5
+    send = pl.pallas_call(
+        lesser_kernel,
+        out_shape=jax.ShapeDtypeStruct((devices, 3, rows, LANES), jnp.bfloat16),
+        grid=(local,),
+        in_specs=[
+            pl.BlockSpec((1, slabs, 3, 2, order, order), lambda e: (e, 0, 0, 0, 0, 0)),
+            pl.BlockSpec((1, slabs, 2, order, order), lambda e: (e, 0, 0, 0, 0)),
+            pl.BlockSpec((1, 1, 2, order, order), lambda e: (e, 0, 0, 0, 0)),
+        ],
+        out_specs=pl.BlockSpec((devices, 3, depth, LANES), lambda e: (0, 0, e, 0)),
+        scratch_shapes=[pltpu.VMEM((3, 2 * order, LANES), jnp.float32)],
+        name="lesser",
+    )(green_ret, sigma_less, halo)
+    got = lax.all_to_all(send, "energy", split_axis=0, concat_axis=0, tiled=True)
+
+    forward, backward, plain = transforms(energies, devices)
+    grid_w = screened.reshape(energies, slabs, 2, owned, order)
+    head, tail = grid_w[..., :LANES], grid_w[..., LANES:]
+    arranged = jnp.stack([head[:, 0], head[:, 1], jnp.concatenate([tail[:, 0], tail[:, 1]], axis=-1)])
+    arranged = arranged.reshape(3, energies, 2, owned * LANES)
+    what = jnp.einsum("pfqe,keqn->kpfn", plain, arranged, precision=lax.Precision.HIGH)
+    what = what.reshape(3, 2 * energies, owned * LANES)
+
+    fresh = pl.pallas_call(
+        convolve_kernel,
+        out_shape=jax.ShapeDtypeStruct((devices, 3, rows, LANES), jnp.bfloat16),
+        grid=(3,),
+        in_specs=[
+            pl.BlockSpec((devices, 1, rows, LANES), lambda k: (0, k, 0, 0)),
+            pl.BlockSpec((1, 2 * energies, owned * LANES), lambda k: (k, 0, 0)),
+            pl.BlockSpec((2, 2 * energies, 2 * energies), lambda k: (0, 0, 0)),
+            pl.BlockSpec((2, 2 * energies, 2 * energies), lambda k: (0, 0, 0)),
+        ],
+        out_specs=pl.BlockSpec((devices, 1, rows, LANES), lambda k: (0, k, 0, 0)),
+        scratch_shapes=[
+            pltpu.VMEM((devices * rows, LANES), jnp.float32),
+            pltpu.VMEM((2 * energies, owned * LANES), jnp.bfloat16),
+        ],
+        name="convolve",
+    )(got, what, forward, backward)
+    back = lax.all_to_all(fresh, "energy", split_axis=0, concat_axis=0, tiled=True)
+
+    out = jax.ShapeDtypeStruct((local, slabs, 2, order, order), jnp.bfloat16)
+    whole_block = pl.BlockSpec((1, slabs, 2, order, order), lambda e: (e, 0, 0, 0, 0))
+    return pl.pallas_call(
+        renew_kernel,
+        out_shape=(out, out),
+        grid=(local,),
+        in_specs=[
+            pl.BlockSpec((devices, 3, depth, LANES), lambda e: (0, 0, e, 0)),
+            pl.BlockSpec((1, slabs, 1, 2, order, order), lambda e: (e, 0, 1, 0, 0, 0)),
+        ],
+        out_specs=(whole_block, whole_block),
+        scratch_shapes=[pltpu.VMEM((3, 2 * order, LANES), jnp.float32)],
+        name="renew",
+    )(back, green_ret)
 
 
 def with_halo(cells, sides, width):
@@ -76,7 +271,7 @@
     return result.astype(jnp.bfloat16)
 
 
-def shards(green_ret, sigma_less, screened):
+def plain_shards(green_ret, sigma_less, screened):
     energy_dev = sigma_less.shape[0]
     slab_dev = sigma_less.shape[1]
     order = sigma_less.shape[-1]
@@ -98,6 +293,20 @@
     return (sigma_new, renewed)
 
 
+def shards(green_ret, sigma_less, screened):
+    order = sigma_less.shape[-1]
+    devices = lax.axis_size("energy")
+    fits = (
+        lax.axis_size("slab") == 2
+        and sigma_less.shape[1] == 2
+        and order == LANES + LANES // 2
+        and order % devices == 0
+        and (2 * order // devices) % 8 == 0
+        and devices % 16 == 0
+    )
+    return (fast_shards if fits else plain_shards)(green_ret, sigma_less, screened)
+
+
 def solution(mesh):
     in_specs = (
         P("energy", "slab", None, None, None, None),

time: 411 us -> 81.5 us (0.20)
  local copies, waits for them, and re-layouts: 308 us -> 11.3 us
  matrix products: 34.3 us -> 2.14 us
  Pallas kernels: 0 us -> 18.5 us
  waiting for transfers between devices: 17.5 us -> 10.7 us
    unnamed x19 -> x11, local copies, waits for them, and re-layouts: 150 us -> 2.48 us
    convert_element_type x2 -> x0, local copies, waits for them, and re-layouts: 66.8 us -> none  [the longest x1 66.1 us: shards(): total.astype(jnp.bfloat16).reshape(energy_dev, slab_dev, 2, order * order)]
    all_to_all x3 -> x0, local copies, waits for them, and re-layouts: 55.1 us -> none  [the longest x2 55 us: shards(): lax.all_to_all(lesser, 'energy', split_axis=3, concat_axis=0, tiled=True)]
    dot_general x35 -> x1, matrix products: 34.3 us -> 2.14 us  [fast_shards(): jnp.einsum('pfqe,keqn->kpfn', plain, arranged, precision=lax.Precision.HIGH)]
    pallas_call x0 -> x3, Pallas kernels: none -> 18.5 us  [the longest x1 8.04 us: fast_shards(): pl.pallas_call(lesser_kernel, out_shape=jax.ShapeDtypeStruct((devices, 3,...]
    another operation x6 -> x3, local copies, waits for them, and re-layouts: 14.7 us -> 3.48 us  [fast_shards(): jnp.stack([head[:, 0], head[:, 1], jnp.concatenate([tail[:, 0], tail[:, 1...]
    all_to_all x1, waiting for transfers between devices: 17.5 us -> 9.05 us  [fast_shards(): lax.all_to_all(send, 'energy', split_axis=0, concat_axis=0, tiled=True)]
    sub x3 -> x0, local copies, waits for them, and re-layouts: 8.25 us -> none  [cmul_plain(): jnp.einsum('...ab,...bc->...ac', lr, rr, preferred_element_type=jnp.float32)]
  transfers between devices with their start and end apart: 3 -> 2, of which waited for: 1 -> 2; matrix products, arithmetic and copies ran while one was open for 6% -> 16% of each run, Pallas kernels for 0% -> 0%
where the time goes in v1:
time: 81.5 us; the launch traced here: 81 us
  blocking collectives  27.6 us (34%)
  Pallas kernels  18.5 us (23%)
  local copies, waits for them, and re-layouts  11.3 us (14%)
  waiting for transfers between devices  10.7 us (13%)
  starting transfers between devices  8.96 us (11%)
  matrix products  2.14 us (3%)
  other arithmetic  1.15 us (1%)
    all_to_all x1, blocking collectives, fast_shards(): lax.all_to_all(fresh, 'energy', split_axis=0, concat_axis=0, tiled=True)  27.6 us
    all_to_all x1, waiting for transfers between devices, fast_shards(): lax.all_to_all(send, 'energy', split_axis=0, concat_axis=0, tiled=True)  9.05 us
    all_to_all x1, starting transfers between devices, fast_shards(): lax.all_to_all(send, 'energy', split_axis=0, concat_axis=0, tiled=True)  8.4 us
    pallas_call x1, Pallas kernels, fast_shards(): pl.pallas_call(lesser_kernel, out_shape=jax.ShapeDtypeStruct((devices, 3,...  8.04 us
    pallas_call x1, Pallas kernels, fast_shards(): pl.pallas_call(renew_kernel, out_shape=(out, out), grid=(local,), in_spec...  5.61 us
    pallas_call x1, Pallas kernels, fast_shards(): pl.pallas_call(convolve_kernel, out_shape=jax.ShapeDtypeStruct((devices,...  4.86 us
    another operation x3, local copies, waits for them, and re-layouts, fast_shards(): jnp.stack([head[:, 0], head[:, 1], jnp.concatenate([tail[:, 0], tail[:, 1...  3.48 us
    reshape x1, local copies, waits for them, and re-layouts, fast_shards(): grid_w = screened.reshape(energies, slabs, 2, owned, order)  2.77 us
  transfers between devices with their start and end apart: 2, of which 2 were waited for; matrix products, arithmetic and copies ran while one was open for 16% of the time, Pallas kernels for 0%

profile of v1, /device:TPU:0, one launch (start us, length us, event | category | flops | bytes accessed | tf_op | source)
XLA Modules:
  0.0 81.0 jit_solution(8618682891877685593)
XLA Ops:
  0.6 1.1 %constant_dynamic-slice_fusion = bf16[3,1,2,192,192]{4,3,2,1,0:T(8,128)(2,1)S(1)} fusion(bf16[3,2,2,192,192]{4,3,2,1,0:T(8,128)(2,1)} %sigma_ref.1, s32[]{:T(128)S(6)} %select_n.3), kind=kLoop, calls=%fused_computation.9 | loop fusion | bytes 884740 | tf_op jit(solution)/shard_map/dynamic_slice | solution.py:143
  1.7 0.6 collective-permute-start
  2.3 1.6 %collective-permute-done.halo_ref = bf16[3,1,2,192,192]{4,3,2,1,0:T(8,128)(2,1)S(1)} collective-permute-done((bf16[3,1,2,192,192]{4,3,2,1,0:T(8,128)(2,1)S(1)}, bf16[3,1,2,192,192]{4,3,2,1,0:T(8,128)(2,1)S(1)}, u32[]{:S(2)}, u32[]{:S(2)}) %collective-permute-start) | collective-permute-done | bytes 442400 | tf_op jit(solution)/shard_map/ppermute | solution.py:142
  3.9 0.0 copy-start.3
  3.9 0.8 %copy-done.3 = bf16[3,1,2,192,192]{4,3,2,1,0:T(8,128)(2,1)} copy-done((bf16[3,1,2,192,192]{4,3,2,1,0:T(8,128)(2,1)}, bf16[3,1,2,192,192]{4,3,2,1,0:T(8,128)(2,1)S(1)}, u32[]{:S(2)}) %copy-start.3) | copy-done | bytes 442392
  4.8 8.0 %lesser.1 = bf16[16,3,72,128]{3,2,1,0:T(8,128)(2,1)} custom-call(bf16[3,2,3,2,192,192]{5,4,3,2,1,0:T(8,128)(2,1)} %green_ref.3, bf16[3,2,2,192,192]{4,3,2,1,0:T(8,128)(2,1)} %sigma_ref.1, bf16[3,1,2,192,192]{4,3,2,1,0:T(8,128)(2,1)} %copy-done.3), custom_call_target="tpu_custom_call" | custom-call | tf_op jit(solution)/shard_map/lesser/pallas_call | solution.py:146
  12.8 0.0 copy-start.2
  12.8 8.4 %all-to-all-start = ((bf16[16,3,72,128]{3,2,1,0:T(8,128)(2,1)}), bf16[16,3,72,128]{3,2,1,0:T(8,128)(2,1)}, u32[]{:S(2)}, u32[]{:S(2)}) async-start(bf16[16,3,72,128]{3,2,1,0:T(8,128)(2,1)} %lesser.1), calls=%async_computation | async-start | bytes 1769472 | tf_op jit(solution)/shard_map/all_to_all | solution.py:159
  21.2 0.0 copy-done.2
  21.2 1.5 %copy.12 = f32[48,2,2,2304]{3,0,2,1:T(8,128)} copy(f32[48,2,2,2304]{3,2,1,0:T(2,128)S(1)} %copy-done.2) | data formatting | bytes 3538944 | tf_op args[2]
  22.8 2.8 %reshape.17 = f32[48,2,2,12,192]{4,3,0,2,1:T(8,128)S(1)} reshape(f32[48,2,2,2304]{3,0,2,1:T(8,128)} %copy.12) | data formatting | bytes 3538944 | tf_op jit(solution)/shard_map/reshape | solution.py:162
  25.5 0.2 slice_bitcast_fusion.1
  25.7 1.2 %pad_maximum_fusion = f32[48,2,12,128]{3,2,0,1:T(8,128)} fusion(f32[48,2,12,64]{3,2,0,1:T(8,128)S(1)} %get-tuple-element.5, f32[48,2,12,64]{3,2,0,1:T(8,128)S(1)} %get-tuple-element.4), kind=kLoop, calls=%fused_computation.8 | loop fusion | flops 147456 | bytes 1179648 | tf_op jit(solution)/shard_map/concatenate | solution.py:164
  26.9 2.1 %stack.12 = f32[1,48,2,1536]{3,1,2,0:T(8,128)} reshape(f32[48,2,12,128]{3,2,0,1:T(8,128)} %pad_maximum_fusion) | data formatting | bytes 1179648 | tf_op jit(solution)/shard_map/stack | solution.py:164
  28.9 1.3 %fusion.6 = (f32[48,1,2,12,128]{4,3,0,2,1:T(8,128)}, f32[48,1,2,12,128]{4,3,0,2,1:T(8,128)}) fusion(f32[48,2,2,12,192]{4,3,0,2,1:T(8,128)S(1)} %reshape.17), kind=kLoop, calls=%fused_computation.11 | loop fusion | bytes 2359296 | tf_op jit(solution)/shard_map/slice | solution.py:164
  30.2 0.0 copy-start
  30.2 0.0 copy-start.1
  30.2 0.0 copy-start.4
  30.2 1.3 %stack.10 = f32[1,48,2,1536]{3,1,2,0:T(8,128)S(1)} reshape(f32[48,1,2,12,128]{4,3,0,2,1:T(8,128)} %get-tuple-element.2) | data formatting | bytes 1179648 | tf_op jit(solution)/shard_map/stack | solution.py:164
  31.6 0.0 copy-done
  31.6 0.1 stack.11
  31.7 0.1 copy-done.1
  31.8 0.0 copy-done.4
  31.8 2.1 %fusion = f32[3,1536,2,48,1]{1,3,4,2,0:T(8,128)} fusion(f32[2,48,2,48,1]{3,1,2,0,4:T(8,128)S(1)} %copy-done.4, f32[1,48,2,1536]{3,1,2,0:T(8,128)S(1)} %copy-done.1, f32[1,48,2,1536]{3,1,2,0:T(8,128)S(1)} %stack.11, f32[1,48,2,1536]{3,1,2,0:T(8,128)S(1)} %stack.10), kind=kOutput, calls=%fused_computation.1 | convolution fusion | flops 255688704 | bytes 3575808 | tf_op jit(solution)/shard_map/pfqe,keqn->kpfn/dot_general | solution.py:166
  33.9 9.0 %all-to-all-done.got_ref = bf16[16,3,72,128]{3,2,1,0:T(8,128)(2,1)} async-done(((bf16[16,3,72,128]{3,2,1,0:T(8,128)(2,1)}), bf16[16,3,72,128]{3,2,1,0:T(8,128)(2,1)}, u32[]{:S(2)}, u32[]{:S(2)}) %all-to-all-start) | async-done | bytes 884768 | tf_op jit(solution)/shard_map/all_to_all | solution.py:159
  43.0 4.9 %convolve.1 = bf16[16,3,72,128]{3,2,1,0:T(8,128)(2,1)} custom-call(bf16[16,3,72,128]{3,2,1,0:T(8,128)(2,1)} %all-to-all-done.got_ref, f32[3,96,1536]{2,1,0:T(8,128)} %bitcast.27, bf16[2,96,96]{2,1,0:T(8,128)(2,1)} %constant.17.clone.fwd_ref, bf16[2,96,96]{2,1,0:T(8,128)(2,1)} %constant.18.clone.bwd_ref), custom_call_target="tpu_custom_call" | custom-call | tf_op jit(solution)/shard_map/convolve/pallas_call | solution.py:169
  47.8 27.6 %all_to_all.10.got_ref = bf16[16,3,72,128]{3,2,1,0:T(8,128)(2,1)} all-to-all(bf16[16,3,72,128]{3,2,1,0:T(8,128)(2,1)} %convolve.1), channel_id=1, replica_groups=mesh['energy'=16,'slab'=2] {'energy'}, dimensions={0} | all-to-all | bytes 1769472 | tf_op jit(solution)/shard_map/all_to_all | solution.py:186
  75.4 5.6 %renew.1 = (bf16[3,2,2,192,192]{4,3,2,1,0:T(8,128)(2,1)}, bf16[3,2,2,192,192]{4,3,2,1,0:T(8,128)(2,1)}) custom-call(bf16[16,3,72,128]{3,2,1,0:T(8,128)(2,1)} %all_to_all.10.got_ref, bf16[3,2,3,2,192,192]{5,4,3,2,1,0:T(8,128)(2,1)} %green_ref.3), custom_call_target="tpu_custom_call" | custom-call | tf_op jit(solution)/shard_map/renew/pallas_call | solution.py:190
Async XLA Ops:
  1.7 2.2 %collective-permute-start = (bf16[3,1,2,192,192]{4,3,2,1,0:T(8,128)(2,1)S(1)}, bf16[3,1,2,192,192]{4,3,2,1,0:T(8,128)(2,1)S(1)}, u32[]{:S(2)}, u32[]{:S(2)}) collective-permute-start(bf16[3,1,2,192,192]{4,3,2,1,0:T(8,128)(2,1)S(1)} %constant_dynamic-slice_fusion), channel_id=1, source_target_pairs={{0,1},{1,0},{2,3},{3,2},{4,5},{5,4},{6,7},{7,6},{8,9},{9,8},{10,11... | collective-permute-start | bytes 1327112 | tf_op jit(solution)/shard_map/ppermute | solution.py:142
  3.9 0.8 %copy-start.3 = (bf16[3,1,2,192,192]{4,3,2,1,0:T(8,128)(2,1)}, bf16[3,1,2,192,192]{4,3,2,1,0:T(8,128)(2,1)S(1)}, u32[]{:S(2)}) copy-start(bf16[3,1,2,192,192]{4,3,2,1,0:T(8,128)(2,1)S(1)} %collective-permute-done.halo_ref) | copy-start | bytes 1327108
  12.8 8.4 %copy-start.2 = (f32[48,2,2,2304]{3,2,1,0:T(2,128)S(1)}, f32[48,2,2,2304]{3,2,1,0:T(2,128)}, u32[]{:S(2)}) copy-start(f32[48,2,2,2304]{3,2,1,0:T(2,128)} %param.8) | copy-start | bytes 5308420
  12.8 30.2 %all-to-all-start = ((bf16[16,3,72,128]{3,2,1,0:T(8,128)(2,1)}), bf16[16,3,72,128]{3,2,1,0:T(8,128)(2,1)}, u32[]{:S(2)}, u32[]{:S(2)}) async-start(bf16[16,3,72,128]{3,2,1,0:T(8,128)(2,1)} %lesser.1), calls=%async_computation | async-start | bytes 1769472 | tf_op jit(solution)/shard_map/all_to_all | solution.py:159
  30.2 1.4 %copy-start = (f32[48,1,2,12,128]{4,3,0,2,1:T(8,128)S(1)}, f32[48,1,2,12,128]{4,3,0,2,1:T(8,128)}, u32[]{:S(2)}) copy-start(f32[48,1,2,12,128]{4,3,0,2,1:T(8,128)} %get-tuple-element.3) | copy-start | bytes 1769476
  30.2 1.5 %copy-start.1 = (f32[1,48,2,1536]{3,1,2,0:T(8,128)S(1)}, f32[1,48,2,1536]{3,1,2,0:T(8,128)}, u32[]{:S(2)}) copy-start(f32[1,48,2,1536]{3,1,2,0:T(8,128)} %stack.12) | copy-start | bytes 1769476
  30.2 1.5 %copy-start.4 = (f32[2,48,2,48,1]{3,1,2,0,4:T(8,128)S(1)}, f32[2,48,2,48,1]{3,1,2,0,4:T(8,128)}, u32[]{:S(2)}) copy-start(f32[2,48,2,48,1]{3,1,2,0,4:T(8,128)} %constant.22) | copy-start | bytes 110596

commit v2 on v0

--- a/solution.py
+++ b/solution.py
@@ -1,9 +1,287 @@
+import functools
 import math
 
 import jax
 import jax.numpy as jnp
+import ml_dtypes
+import numpy as np
 from jax import lax
+from jax.experimental import pallas as pl
+from jax.experimental.pallas import tpu as pltpu
 from jax.sharding import PartitionSpec as P
+
+LANES = 128
+NT = (((1,), (1,)), ((), ()))
+NN = (((1,), (0,)), ((), ()))
+
+
+def dot(left, right, dims):
+    return lax.dot_general(left, right, dims, preferred_element_type=jnp.float32)
+
+
+def inner_parts(green, sigma):
+    real = dot(sigma[0], green[0], NT) + dot(sigma[1], green[1], NT)
+    imag = dot(sigma[1], green[0], NT) + dot(sigma[0], -green[1], NT)
+    return real.astype(jnp.bfloat16), imag.astype(jnp.bfloat16)
+
+
+def outer_parts(green, inner):
+    real, imag = inner
+    return (
+        dot(green[0], real, NN) + dot(-green[1], imag, NN),
+        dot(green[0], imag, NN) + dot(green[1], real, NN),
+    )
+
+
+def congruence(green, sigma):
+    return outer_parts(green, inner_parts(green, sigma))
+
+
+def edge_place(slab_axis):
+    first = lax.axis_index(slab_axis) == 0
+    return jnp.where(first, 1, 0), jnp.where(first, 2, 0)
+
+
+def near_kernel(green_hbm, sigma_hbm, total_ref, edge_ref, green, sigma, sems):
+    local = green.shape[0]
+    edge_slab, edge_block = edge_place("slab")
+    copies = []
+    for energy in range(local):
+        copies.append(
+            [
+                pltpu.make_async_copy(sigma_hbm.at[energy], sigma.at[energy], sems.at[energy, 0]),
+                pltpu.make_async_copy(
+                    green_hbm.at[energy, 0, pl.ds(1, 2)], green.at[energy, 0], sems.at[energy, 1]
+                ),
+                pltpu.make_async_copy(
+                    green_hbm.at[energy, 1, pl.ds(0, 2)], green.at[energy, 1], sems.at[energy, 2]
+                ),
+            ]
+        )
+    edges = [
+        pltpu.make_async_copy(
+            green_hbm.at[energy, edge_slab, edge_block], edge_ref.at[energy], sems.at[energy, 3]
+        )
+        for energy in range(local)
+    ]
+    for group in copies:
+        for copy in group:
+            copy.start()
+    for copy in edges:
+        copy.start()
+    for energy in range(local):
+        for copy in copies[energy]:
+            copy.wait()
+        for slab in range(2):
+            terms = [
+                congruence(green[energy, slab, source], sigma[energy, source]) for source in range(2)
+            ]
+            for part in range(2):
+                total_ref[energy, slab, part] = terms[0][part] + terms[1][part]
+    for copy in edges:
+        copy.wait()
+
+
+def far_kernel(total_ref, edge_ref, halo_ref, out_ref, stage):
+    local, _, _, order, _ = total_ref.shape
+    devices, blocks, rows, _ = out_ref.shape
+    depth = rows // local
+    edge_slab, _ = edge_place("slab")
+    other = 1 - edge_slab
+    for energy in range(local):
+        far = congruence(edge_ref[energy], halo_ref[energy, other])
+        for part in range(2):
+            one, two = [
+                total_ref[energy, slab, part] + jnp.where(edge_slab == slab, far[part], 0.0)
+                for slab in range(2)
+            ]
+            at = pl.ds(part, order, stride=2)
+            stage[energy, 0, at, :] = one[:, :LANES]
+            stage[energy, 1, at, :] = two[:, :LANES]
+            stage[energy, 2, at, :] = jnp.concatenate([one[:, LANES:], two[:, LANES:]], axis=1)
+        for block in range(blocks):
+            out_ref[:, block, energy * depth : (energy + 1) * depth] = (
+                stage[energy, block].reshape(devices, depth, LANES).astype(jnp.bfloat16)
+            )
+
+
+def convolve_kernel(got_ref, what_ref, fwd_ref, bwd_ref, out_ref, stage, packed):
+    devices, blocks, rows, _ = got_ref.shape
+    half = fwd_ref.shape[0] // 2
+    local = half // devices
+    depth = rows // local
+    owned = depth // 2
+    for block in range(blocks):
+        flat = stage.at[block]
+        flat[...] = got_ref[:, block].astype(jnp.float32).reshape(devices * rows, LANES)
+        for row in range(owned):
+            for part in range(2):
+                for energy in range(local):
+                    picked = flat[pl.ds(energy * depth + row * 2 + part, devices, stride=rows), :]
+                    at = part * half + energy * devices
+                    packed[block, at : at + devices, row * LANES : (row + 1) * LANES] = picked.astype(
+                        jnp.bfloat16
+                    )
+        held = packed[block]
+        ghat = dot(fwd_ref[...], jnp.concatenate([held, held], axis=0), NN)
+        what = what_ref[block]
+        real = ghat[:half] * what[:half] - ghat[half:] * what[half:]
+        imag = ghat[:half] * what[half:] + ghat[half:] * what[:half]
+        product = jnp.concatenate([real, imag], axis=0).astype(jnp.bfloat16)
+        result = dot(bwd_ref[...], jnp.concatenate([product, product], axis=0), NN)
+        for row in range(owned):
+            for part in range(2):
+                for energy in range(local):
+                    at = part * half + energy * devices
+                    flat[pl.ds(energy * depth + row * 2 + part, devices, stride=rows), :] = result[
+                        at : at + devices, row * LANES : (row + 1) * LANES
+                    ]
+        out_ref[:, block] = flat[...].reshape(devices, rows, LANES).astype(jnp.bfloat16)
+
+
+def renew_kernel(got_ref, green_ref, sigma_hbm, renewed_hbm, stage, sigma, renewed, sems):
+    local, _, _, order, _ = sigma.shape
+    rows = got_ref.shape[2]
+    depth = rows // local
+    rest = order - LANES
+    copies = []
+    for energy in range(local):
+        for block in range(3):
+            stage[energy, block] = (
+                got_ref[:, block, energy * depth : (energy + 1) * depth]
+                .astype(jnp.float32)
+                .reshape(2 * order, LANES)
+            )
+        for part in range(2):
+            at = pl.ds(part, order, stride=2)
+            mixed = stage[energy, 2, at, :]
+            sigma[energy, 0, part, :, :LANES] = stage[energy, 0, at, :].astype(jnp.bfloat16)
+            sigma[energy, 1, part, :, :LANES] = stage[energy, 1, at, :].astype(jnp.bfloat16)
+            sigma[energy, 0, part, :, LANES:] = mixed[:, :rest].astype(jnp.bfloat16)
+            sigma[energy, 1, part, :, LANES:] = pltpu.roll(mixed, rest, 1)[:, :rest].astype(jnp.bfloat16)
+        copies.append(pltpu.make_async_copy(sigma.at[energy], sigma_hbm.at[energy], sems.at[energy, 0]))
+        copies[-1].start()
+        for slab in range(2):
+            fresh = congruence(green_ref[energy, slab, 0], sigma[energy, slab])
+            for part in range(2):
+                renewed[energy, slab, part] = fresh[part].astype(jnp.bfloat16)
+            copies.append(
+                pltpu.make_async_copy(
+                    renewed.at[energy, slab], renewed_hbm.at[energy, slab], sems.at[energy, 1 + slab]
+                )
+            )
+            copies[-1].start()
+    for copy in copies:
+        copy.wait()
+
+
+def split_high_low(matrix):
+    high = matrix.astype(ml_dtypes.bfloat16)
+    low = (matrix - high.astype(np.float64)).astype(ml_dtypes.bfloat16)
+    return jnp.asarray(np.concatenate([high, low], axis=1))
+
+
+def transforms(energies, devices):
+    local = energies // devices
+    index = np.arange(energies)
+    angle = (index[:, None] * index[None, :] % energies) * (2.0 * math.pi / energies)
+    cosine, sine = np.cos(angle), np.sin(angle)
+    order = (np.arange(devices)[None, :] * local + np.arange(local)[:, None]).reshape(-1)
+    scale = 1.0 / (energies * math.sqrt(energies))
+    forward = np.block([[cosine[:, order], sine[:, order]], [-sine[:, order], cosine[:, order]]])
+    backward = scale * np.block([[cosine[order], -sine[order]], [sine[order], cosine[order]]])
+    plain = np.stack([np.stack([cosine, sine], 1), np.stack([-sine, cosine], 1)])
+    return split_high_low(forward), split_high_low(backward), jnp.asarray(plain, jnp.float32)
+
+
+def vmem(array):
+    return pltpu.with_memory_space_constraint(array, pltpu.VMEM)
+
+
+def hbm(array):
+    return pltpu.with_memory_space_constraint(array, pltpu.HBM)
+
+
+IN_VMEM = pl.BlockSpec(memory_space=pltpu.VMEM)
+IN_HBM = pl.BlockSpec(memory_space=pltpu.HBM)
+GRANT = pltpu.CompilerParams(vmem_limit_bytes=20 << 20)
+
+
+def fast_shards(green_ret, sigma_less, screened):
+    devices = lax.axis_size("energy")
+    local, slabs, _, order, _ = sigma_less.shape
+    energies = local * devices
+    owned = order // devices
+    depth = 2 * owned
+    rows = depth * local
+    sent = pltpu.VMEM((devices, 3, rows, LANES), jnp.bfloat16)
+    dma = pltpu.SemaphoreType.DMA
+
+    halo = lax.ppermute(sigma_less, "slab", [(0, 1), (1, 0)])
+    total, edge = pl.pallas_call(
+        near_kernel,
+        out_shape=(
+            pltpu.VMEM((local, slabs, 2, order, order), jnp.float32),
+            pltpu.VMEM((local, 2, order, order), jnp.bfloat16),
+        ),
+        in_specs=[IN_HBM, IN_HBM],
+        out_specs=(IN_VMEM, IN_VMEM),
+        scratch_shapes=[
+            pltpu.VMEM((local, slabs, 2, 2, order, order), jnp.bfloat16),
+            pltpu.VMEM((local, slabs, 2, order, order), jnp.bfloat16),
+            dma((local, 4)),
+        ],
+        compiler_params=GRANT,
+        name="near",
+    )(hbm(green_ret), hbm(sigma_less))
+    send = pl.pallas_call(
+        far_kernel,
+        out_shape=sent,
+        in_specs=[IN_VMEM] * 3,
+        out_specs=IN_VMEM,
+        scratch_shapes=[pltpu.VMEM((local, 3, 2 * order, LANES), jnp.float32)],
+        compiler_params=GRANT,
+        name="far",
+    )(vmem(total), vmem(edge), vmem(halo))
+    got = lax.all_to_all(send, "energy", split_axis=0, concat_axis=0, tiled=True)
+
+    forward, backward, plain = transforms(energies, devices)
+    grid_w = screened.reshape(energies, slabs, 2, owned, order)
+    head, tail = grid_w[..., :LANES], grid_w[..., LANES:]
+    arranged = jnp.stack([head[:, 0], head[:, 1], jnp.concatenate([tail[:, 0], tail[:, 1]], axis=-1)])
+    arranged = arranged.reshape(3, energies, 2, owned * LANES)
+    what = jnp.einsum("pfqe,keqn->kpfn", plain, arranged, precision=lax.Precision.HIGH)
+    what = what.reshape(3, 2 * energies, owned * LANES)
+
+    fresh = pl.pallas_call(
+        convolve_kernel,
+        out_shape=sent,
+        in_specs=[IN_VMEM] * 4,
+        out_specs=IN_VMEM,
+        scratch_shapes=[
+            pltpu.VMEM((3, devices * rows, LANES), jnp.float32),
+            pltpu.VMEM((3, 2 * energies, owned * LANES), jnp.bfloat16),
+        ],
+        compiler_params=GRANT,
+        name="convolve",
+    )(vmem(got), vmem(what), vmem(forward), vmem(backward))
+    back = lax.all_to_all(fresh, "energy", split_axis=0, concat_axis=0, tiled=True)
+
+    out = jax.ShapeDtypeStruct((local, slabs, 2, order, order), jnp.bfloat16)
+    return pl.pallas_call(
+        renew_kernel,
+        out_shape=(out, out),
+        in_specs=[IN_VMEM] * 2,
+        out_specs=(IN_HBM, IN_HBM),
+        scratch_shapes=[
+            pltpu.VMEM((local, 3, 2 * order, LANES), jnp.float32),
+            pltpu.VMEM((local, slabs, 2, order, order), jnp.bfloat16),
+            pltpu.VMEM((local, slabs, 2, order, order), jnp.bfloat16),
+            dma((local, 3)),
+        ],
+        compiler_params=GRANT,
+        name="renew",
+    )(vmem(back), vmem(green_ret[:, :, 1:2]))
 
 
 def with_halo(cells, sides, width):
@@ -76,7 +354,7 @@
     return result.astype(jnp.bfloat16)
 
 
-def shards(green_ret, sigma_less, screened):
+def plain_shards(green_ret, sigma_less, screened):
     energy_dev = sigma_less.shape[0]
     slab_dev = sigma_less.shape[1]
     order = sigma_less.shape[-1]
@@ -98,6 +376,20 @@
     return (sigma_new, renewed)
 
 
+def shards(green_ret, sigma_less, screened):
+    order = sigma_less.shape[-1]
+    devices = lax.axis_size("energy")
+    fits = (
+        lax.axis_size("slab") == 2
+        and sigma_less.shape[1] == 2
+        and order == LANES + LANES // 2
+        and order % devices == 0
+        and (2 * order // devices) % 8 == 0
+        and devices % 16 == 0
+    )
+    return (fast_shards if fits else plain_shards)(green_ret, sigma_less, screened)
+
+
 def solution(mesh):
     in_specs = (
         P("energy", "slab", None, None, None, None),

time: 411 us -> 71.6 us (0.17)
  local copies, waits for them, and re-layouts: 308 us -> 10.5 us
  matrix products: 34.3 us -> 2.16 us
  blocking collectives: 31.4 us -> 0 us
  Pallas kernels: 0 us -> 13.7 us
  waiting for transfers between devices: 17.5 us -> 29.5 us
    unnamed x19 -> x7, local copies, waits for them, and re-layouts: 150 us -> 1.84 us
    convert_element_type x2 -> x0, local copies, waits for them, and re-layouts: 66.8 us -> none  [the longest x1 66.1 us: shards(): total.astype(jnp.bfloat16).reshape(energy_dev, slab_dev, 2, order * order)]
    all_to_all x3 -> x0, local copies, waits for them, and re-layouts: 55.1 us -> none  [the longest x2 55 us: shards(): lax.all_to_all(lesser, 'energy', split_axis=3, concat_axis=0, tiled=True)]
    dot_general x35 -> x1, matrix products: 34.3 us -> 2.16 us  [fast_shards(): jnp.einsum('pfqe,keqn->kpfn', plain, arranged, precision=lax.Precision.HIGH)]
    all_to_all x1 -> x0, blocking collectives: 31.4 us -> none  [shards(): lax.all_to_all(fresh, 'energy', split_axis=0, concat_axis=3, tiled=True)]
    pallas_call x0 -> x4, Pallas kernels: none -> 13.7 us  [the longest x1 5.94 us: fast_shards(): pl.pallas_call(near_kernel, out_shape=(pltpu.VMEM((local, slabs, 2, order...]
    another operation x6 -> x3, local copies, waits for them, and re-layouts: 14.7 us -> 1.89 us  [fast_shards(): jnp.stack([head[:, 0], head[:, 1], jnp.concatenate([tail[:, 0], tail[:, 1...]
    all_to_all x1 -> x2, waiting for transfers between devices: 17.5 us -> 29.5 us  [the longest x1 19.3 us: fast_shards(): lax.all_to_all(fresh, 'energy', split_axis=0, concat_axis=0, tiled=True)]
  transfers between devices with their start and end apart: 3 -> 3, of which waited for: 1 -> 2; matrix products, arithmetic and copies ran while one was open for 6% -> 18% of each run, Pallas kernels for 0% -> 8%
where the time goes in v2:
time: 71.6 us; the launch traced here: 71.1 us
  waiting for transfers between devices  29.5 us (41%)
  starting transfers between devices  14.4 us (20%)
  Pallas kernels  13.7 us (19%)
  local copies, waits for them, and re-layouts  10.5 us (15%)
  matrix products  2.16 us (3%)
    all_to_all x1, waiting for transfers between devices, fast_shards(): lax.all_to_all(fresh, 'energy', split_axis=0, concat_axis=0, tiled=True)  19.3 us
    all_to_all x1, waiting for transfers between devices, fast_shards(): lax.all_to_all(send, 'energy', split_axis=0, concat_axis=0, tiled=True)  10.2 us
    all_to_all x1, starting transfers between devices, fast_shards(): lax.all_to_all(send, 'energy', split_axis=0, concat_axis=0, tiled=True)  7.87 us
    all_to_all x1, starting transfers between devices, fast_shards(): lax.all_to_all(fresh, 'energy', split_axis=0, concat_axis=0, tiled=True)  5.95 us
    pallas_call x1, Pallas kernels, fast_shards(): pl.pallas_call(near_kernel, out_shape=(pltpu.VMEM((local, slabs, 2, order...  5.94 us
    pallas_call x1, Pallas kernels, fast_shards(): pl.pallas_call(renew_kernel, out_shape=(out, out), in_specs=[IN_VMEM] * 2...  3.06 us
    reshape x1, local copies, waits for them, and re-layouts, fast_shards(): grid_w = screened.reshape(energies, slabs, 2, owned, order)  2.44 us
    pallas_call x1, Pallas kernels, fast_shards(): pl.pallas_call(far_kernel, out_shape=sent, in_specs=[IN_VMEM] * 3, out_sp...  2.33 us
  transfers between devices with their start and end apart: 3, of which 2 were waited for; matrix products, arithmetic and copies ran while one was open for 18% of the time, Pallas kernels for 8%

profile of v2, /device:TPU:0, one launch (start us, length us, event | category | flops | bytes accessed | tf_op | source)
XLA Modules:
  0.0 71.1 jit_solution(16858646749712348147)
XLA Ops:
  0.6 0.6 collective-permute-start
  1.2 5.9 %near.1 = (f32[3,2,2,192,192]{4,3,2,1,0:T(8,128)S(1)}, bf16[3,2,192,192]{3,2,1,0:T(8,128)(2,1)S(1)}) custom-call(bf16[3,2,3,2,192,192]{5,4,3,2,1,0:T(8,128)(2,1)} %green_hbm.1, bf16[3,2,2,192,192]{4,3,2,1,0:T(8,128)(2,1)} %sigma_hbm.1), custom_call_target="tpu_custom_call" | custom-call | tf_op jit(solution)/shard_map/near/pallas_call | solution.py:221
  7.1 0.0 collective-permute-done.halo_ref
  7.1 2.3 %far.1 = bf16[16,3,72,128]{3,2,1,0:T(8,128)(2,1)} custom-call(f32[3,2,2,192,192]{4,3,2,1,0:T(8,128)S(1)} %get-tuple-element.4.total_ref, bf16[3,2,192,192]{3,2,1,0:T(8,128)(2,1)S(1)} %get-tuple-element.5.edge_ref, bf16[3,2,2,192,192]{4,3,2,1,0:T(8,128)(2,1)S(1)} %collective-permute-done.halo_ref), custom_call_target="tpu_custom_call" | custom-call | tf_op jit(solution)/shard_map/far/pallas_call | solution.py:237
  9.5 7.9 %all-to-all-start = ((bf16[16,3,72,128]{3,2,1,0:T(8,128)(2,1)}), bf16[16,3,72,128]{3,2,1,0:T(8,128)(2,1)S(1)}, u32[]{:S(2)}, u32[]{:S(2)}) async-start(bf16[16,3,72,128]{3,2,1,0:T(8,128)(2,1)} %far.1), calls=%async_computation | async-start | bytes 1769472 | tf_op jit(solution)/shard_map/all_to_all | solution.py:246
  17.3 1.8 %copy.12 = f32[48,2,2,2304]{3,0,2,1:T(8,128)S(1)} copy(f32[48,2,2,2304]{3,2,1,0:T(2,128)} %param.8) | data formatting | bytes 3538944 | tf_op args[2]
  19.2 2.4 %reshape.17 = f32[48,2,2,12,192]{4,3,0,2,1:T(8,128)} reshape(f32[48,2,2,2304]{3,0,2,1:T(8,128)S(1)} %copy.12) | data formatting | bytes 3538944 | tf_op jit(solution)/shard_map/reshape | solution.py:249
  21.6 1.5 %slice_bitcast_fusion.1 = (f32[48,2,12,64]{3,2,0,1:T(8,128)S(1)}, f32[48,2,12,64]{3,2,0,1:T(8,128)S(1)}) fusion(f32[48,2,2,12,192]{4,3,0,2,1:T(8,128)} %reshape.17), kind=kLoop, calls=%fused_computation.7 | loop fusion | bytes 1179648 | tf_op jit(solution)/shard_map/squeeze | solution.py:251
  23.1 0.3 pad_maximum_fusion
  23.4 0.1 stack.12
  23.5 1.5 %fusion.6 = (f32[48,1,2,12,128]{4,3,0,2,1:T(8,128)S(1)}, f32[48,1,2,12,128]{4,3,0,2,1:T(8,128)S(1)}) fusion(f32[48,2,2,12,192]{4,3,0,2,1:T(8,128)} %reshape.17), kind=kLoop, calls=%fused_computation.10 | loop fusion | bytes 2359296 | tf_op jit(solution)/shard_map/slice | solution.py:251
  24.9 0.0 copy-start.2
  24.9 0.9 %stack.11 = f32[1,48,2,1536]{3,1,2,0:T(8,128)} reshape(f32[48,1,2,12,128]{4,3,0,2,1:T(8,128)S(1)} %get-tuple-element.7) | data formatting | bytes 1179648 | tf_op jit(solution)/shard_map/stack | solution.py:251
  25.9 0.9 %stack.10 = f32[1,48,2,1536]{3,1,2,0:T(8,128)} reshape(f32[48,1,2,12,128]{4,3,0,2,1:T(8,128)S(1)} %get-tuple-element.6) | data formatting | bytes 1179648 | tf_op jit(solution)/shard_map/stack | solution.py:251
  26.8 0.0 copy-done.2
  26.8 0.0 copy-start
  26.8 0.0 copy-start.1
  26.8 2.2 %fusion = f32[3,1536,2,48,1]{1,3,4,2,0:T(8,128)S(1)} fusion(f32[2,48,2,48,1]{3,1,2,0,4:T(8,128)S(1)} %copy-done.2, f32[1,48,2,1536]{3,1,2,0:T(8,128)S(1)} %stack.12, f32[1,48,2,1536]{3,1,2,0:T(8,128)} %stack.11, f32[1,48,2,1536]{3,1,2,0:T(8,128)} %stack.10), kind=kOutput, calls=%fused_computation.1 | convolution fusion | flops 255688704 | bytes 3575808 | tf_op jit(solution)/shard_map/pfqe,keqn->kpfn/dot_general | solution.py:253
  28.9 10.2 %all-to-all-done.got_ref = bf16[16,3,72,128]{3,2,1,0:T(8,128)(2,1)S(1)} async-done(((bf16[16,3,72,128]{3,2,1,0:T(8,128)(2,1)}), bf16[16,3,72,128]{3,2,1,0:T(8,128)(2,1)S(1)}, u32[]{:S(2)}, u32[]{:S(2)}) %all-to-all-start) | async-done | bytes 884768 | tf_op jit(solution)/shard_map/all_to_all | solution.py:246
  39.2 0.0 copy-done
  39.2 0.0 copy-done.1
  39.2 2.3 %convolve.1 = bf16[16,3,72,128]{3,2,1,0:T(8,128)(2,1)} custom-call(bf16[16,3,72,128]{3,2,1,0:T(8,128)(2,1)S(1)} %all-to-all-done.got_ref, f32[3,96,1536]{2,1,0:T(8,128)S(1)} %bitcast.27, bf16[96,192]{1,0:T(8,128)(2,1)S(1)} %copy-done, bf16[96,192]{1,0:T(8,128)(2,1)S(1)} %copy-done.1), custom_call_target="tpu_custom_call" | custom-call | tf_op jit(solution)/shard_map/convolve/pallas_call | solution.py:256
  41.5 5.9 %all-to-all-start.1 = ((bf16[16,3,72,128]{3,2,1,0:T(8,128)(2,1)}), bf16[16,3,72,128]{3,2,1,0:T(8,128)(2,1)S(1)}, u32[]{:S(2)}, u32[]{:S(2)}) async-start(bf16[16,3,72,128]{3,2,1,0:T(8,128)(2,1)} %convolve.1), calls=%async_computation.1 | async-start | bytes 1769472 | tf_op jit(solution)/shard_map/all_to_all | solution.py:268
  47.4 1.4 %slice.25.green_ref = bf16[3,2,1,2,192,192]{5,4,3,2,1,0:T(8,128)(2,1)S(1)} slice(bf16[3,2,3,2,192,192]{5,4,3,2,1,0:T(8,128)(2,1)} %green_hbm.1), slice={[0:3], [0:2], [1:2], [0:2], [0:192], [0:192]} | slice | bytes 1769472 | tf_op jit(solution)/shard_map/slice | solution.py:284
  48.8 19.3 %all-to-all-done.1.got_ref = bf16[16,3,72,128]{3,2,1,0:T(8,128)(2,1)S(1)} async-done(((bf16[16,3,72,128]{3,2,1,0:T(8,128)(2,1)}), bf16[16,3,72,128]{3,2,1,0:T(8,128)(2,1)S(1)}, u32[]{:S(2)}, u32[]{:S(2)}) %all-to-all-start.1) | async-done | bytes 884768 | tf_op jit(solution)/shard_map/all_to_all | solution.py:268
  68.1 3.1 %renew.1 = (bf16[3,2,2,192,192]{4,3,2,1,0:T(8,128)(2,1)}, bf16[3,2,2,192,192]{4,3,2,1,0:T(8,128)(2,1)}) custom-call(bf16[16,3,72,128]{3,2,1,0:T(8,128)(2,1)S(1)} %all-to-all-done.1.got_ref, bf16[3,2,1,2,192,192]{5,4,3,2,1,0:T(8,128)(2,1)S(1)} %slice.25.green_ref), custom_call_target="tpu_custom_call" | custom-call | tf_op jit(solution)/shard_map/renew/pallas_call | solution.py:271
Async XLA Ops:
  0.6 6.5 %collective-permute-start = (bf16[3,2,2,192,192]{4,3,2,1,0:T(8,128)(2,1)}, bf16[3,2,2,192,192]{4,3,2,1,0:T(8,128)(2,1)S(1)}, u32[]{:S(2)}, u32[]{:S(2)}) collective-permute-start(bf16[3,2,2,192,192]{4,3,2,1,0:T(8,128)(2,1)} %sigma_hbm.1), channel_id=1, source_target_pairs={{0,1},{1,0},{2,3},{3,2},{4,5},{5,4},{6,7},{7,6},{8,9},{9,8},{10,11... | collective-permute-start | bytes 2654216 | tf_op jit(solution)/shard_map/ppermute | solution.py:220
  9.5 29.7 %all-to-all-start = ((bf16[16,3,72,128]{3,2,1,0:T(8,128)(2,1)}), bf16[16,3,72,128]{3,2,1,0:T(8,128)(2,1)S(1)}, u32[]{:S(2)}, u32[]{:S(2)}) async-start(bf16[16,3,72,128]{3,2,1,0:T(8,128)(2,1)} %far.1), calls=%async_computation | async-start | bytes 1769472 | tf_op jit(solution)/shard_map/all_to_all | solution.py:246
  24.9 1.8 %copy-start.2 = (f32[2,48,2,48,1]{3,1,2,0,4:T(8,128)S(1)}, f32[2,48,2,48,1]{3,1,2,0,4:T(8,128)}, u32[]{:S(2)}) copy-start(f32[2,48,2,48,1]{3,1,2,0,4:T(8,128)} %constant.11) | copy-start | bytes 110596
  26.8 12.4 %copy-start = (bf16[96,192]{1,0:T(8,128)(2,1)S(1)}, bf16[96,192]{1,0:T(8,128)(2,1)}, u32[]{:S(2)}) copy-start(bf16[96,192]{1,0:T(8,128)(2,1)} %constant.6.clone.fwd_ref) | copy-start | bytes 110596
  26.8 12.4 %copy-start.1 = (bf16[96,192]{1,0:T(8,128)(2,1)S(1)}, bf16[96,192]{1,0:T(8,128)(2,1)}, u32[]{:S(2)}) copy-start(bf16[96,192]{1,0:T(8,128)(2,1)} %constant.7.clone.bwd_ref) | copy-start | bytes 110596
  41.5 26.6 %all-to-all-start.1 = ((bf16[16,3,72,128]{3,2,1,0:T(8,128)(2,1)}), bf16[16,3,72,128]{3,2,1,0:T(8,128)(2,1)S(1)}, u32[]{:S(2)}, u32[]{:S(2)}) async-start(bf16[16,3,72,128]{3,2,1,0:T(8,128)(2,1)} %convolve.1), calls=%async_computation.1 | async-start | bytes 1769472 | tf_op jit(solution)/shard_map/all_to_all | solution.py:268

commit v3 on v2

--- a/solution.py
+++ b/solution.py
@@ -70,14 +70,28 @@
     for copy in edges:
         copy.start()
     for energy in range(local):
-        for copy in copies[energy]:
-            copy.wait()
+        copies[energy][0].wait()
+        inner = []
         for slab in range(2):
-            terms = [
-                congruence(green[energy, slab, source], sigma[energy, source]) for source in range(2)
-            ]
-            for part in range(2):
-                total_ref[energy, slab, part] = terms[0][part] + terms[1][part]
+            copies[energy][1 + slab].wait()
+            inner.append(
+                [inner_parts(green[energy, slab, source], sigma[energy, source]) for source in range(2)]
+            )
+        for slab in range(2):
+            one, two = green[energy, slab, 0], green[energy, slab, 1]
+            near, next_ = inner[slab]
+            total_ref[energy, slab, 0] = (
+                dot(one[0], near[0], NN)
+                + dot(two[0], next_[0], NN)
+                + dot(-one[1], near[1], NN)
+                + dot(-two[1], next_[1], NN)
+            )
+            total_ref[energy, slab, 1] = (
+                dot(one[0], near[1], NN)
+                + dot(two[0], next_[1], NN)
+                + dot(one[1], near[0], NN)
+                + dot(two[1], next_[0], NN)
+            )
     for copy in edges:
         copy.wait()
 
@@ -88,8 +102,9 @@
     depth = rows // local
     edge_slab, _ = edge_place("slab")
     other = 1 - edge_slab
+    inner = [inner_parts(edge_ref[energy], halo_ref[energy, other]) for energy in range(local)]
     for energy in range(local):
-        far = congruence(edge_ref[energy], halo_ref[energy, other])
+        far = outer_parts(edge_ref[energy], inner[energy])
         for part in range(2):
             one, two = [
                 total_ref[energy, slab, part] + jnp.where(edge_slab == slab, far[part], 0.0)
@@ -105,38 +120,40 @@
             )
 
 
-def convolve_kernel(got_ref, what_ref, fwd_ref, bwd_ref, out_ref, stage, packed):
+def convolve_kernel(got_ref, what_ref, fwd_ref, bwd_ref, out_ref, stage, result):
     devices, blocks, rows, _ = got_ref.shape
     half = fwd_ref.shape[0] // 2
     local = half // devices
     depth = rows // local
     owned = depth // 2
+    width = 2
+
+    def place(block, row, part, energy):
+        return block, pl.ds(energy * depth + row * 2 + part, devices, stride=rows), slice(None)
+
+    each = [(part, energy) for part in range(2) for energy in range(local)]
     for block in range(blocks):
-        flat = stage.at[block]
-        flat[...] = got_ref[:, block].astype(jnp.float32).reshape(devices * rows, LANES)
-        for row in range(owned):
-            for part in range(2):
-                for energy in range(local):
-                    picked = flat[pl.ds(energy * depth + row * 2 + part, devices, stride=rows), :]
-                    at = part * half + energy * devices
-                    packed[block, at : at + devices, row * LANES : (row + 1) * LANES] = picked.astype(
-                        jnp.bfloat16
-                    )
-        held = packed[block]
-        ghat = dot(fwd_ref[...], jnp.concatenate([held, held], axis=0), NN)
-        what = what_ref[block]
-        real = ghat[:half] * what[:half] - ghat[half:] * what[half:]
-        imag = ghat[:half] * what[half:] + ghat[half:] * what[:half]
-        product = jnp.concatenate([real, imag], axis=0).astype(jnp.bfloat16)
-        result = dot(bwd_ref[...], jnp.concatenate([product, product], axis=0), NN)
-        for row in range(owned):
-            for part in range(2):
-                for energy in range(local):
-                    at = part * half + energy * devices
-                    flat[pl.ds(energy * depth + row * 2 + part, devices, stride=rows), :] = result[
-                        at : at + devices, row * LANES : (row + 1) * LANES
+        stage[block] = got_ref[:, block].astype(jnp.float32).reshape(devices * rows, LANES)
+        for start in range(0, owned, width):
+            held = jnp.concatenate(
+                [
+                    jnp.concatenate([stage[place(block, row, *at)] for at in each], axis=0)
+                    for row in range(start, start + width)
+                ],
+                axis=1,
+            ).astype(jnp.bfloat16)
+            ghat = dot(fwd_ref[...], jnp.concatenate([held, held], axis=0), NN)
+            what = what_ref[block, :, start * LANES : (start + width) * LANES]
+            real = ghat[:half] * what[:half] - ghat[half:] * what[half:]
+            imag = ghat[:half] * what[half:] + ghat[half:] * what[:half]
+            product = jnp.concatenate([real, imag], axis=0).astype(jnp.bfloat16)
+            fresh = dot(bwd_ref[...], jnp.concatenate([product, product], axis=0), NN)
+            for offset in range(width):
+                for index, at in enumerate(each):
+                    result[place(block, start + offset, *at)] = fresh[
+                        index * devices : (index + 1) * devices, offset * LANES : (offset + 1) * LANES
                     ]
-        out_ref[:, block] = flat[...].reshape(devices, rows, LANES).astype(jnp.bfloat16)
+        out_ref[:, block] = result[block].reshape(devices, rows, LANES).astype(jnp.bfloat16)
 
 
 def renew_kernel(got_ref, green_ref, sigma_hbm, renewed_hbm, stage, sigma, renewed, sems):
@@ -145,6 +162,7 @@
     depth = rows // local
     rest = order - LANES
     copies = []
+    inner = []
     for energy in range(local):
         for block in range(3):
             stage[energy, block] = (
@@ -161,8 +179,10 @@
             sigma[energy, 1, part, :, LANES:] = pltpu.roll(mixed, rest, 1)[:, :rest].astype(jnp.bfloat16)
         copies.append(pltpu.make_async_copy(sigma.at[energy], sigma_hbm.at[energy], sems.at[energy, 0]))
         copies[-1].start()
+        inner.append([inner_parts(green_ref[energy, slab, 0], sigma[energy, slab]) for slab in range(2)])
+    for energy in range(local):
         for slab in range(2):
-            fresh = congruence(green_ref[energy, slab, 0], sigma[energy, slab])
+            fresh = outer_parts(green_ref[energy, slab, 0], inner[energy][slab])
             for part in range(2):
                 renewed[energy, slab, part] = fresh[part].astype(jnp.bfloat16)
             copies.append(
@@ -260,7 +280,7 @@
         out_specs=IN_VMEM,
         scratch_shapes=[
             pltpu.VMEM((3, devices * rows, LANES), jnp.float32),
-            pltpu.VMEM((3, 2 * energies, owned * LANES), jnp.bfloat16),
+            pltpu.VMEM((3, devices * rows, LANES), jnp.float32),
         ],
         compiler_params=GRANT,
         name="convolve",

time: 71.6 us -> 68.9 us (0.962)
  Pallas kernels: 13.7 us -> 10.9 us
    pallas_call x1, Pallas kernels: 5.94 us -> 4.78 us  [fast_shards(): pl.pallas_call(near_kernel, out_shape=(pltpu.VMEM((local, slabs, 2, order...]
    pallas_call x1, Pallas kernels: 3.06 us -> 2.28 us  [fast_shards(): pl.pallas_call(renew_kernel, out_shape=(out, out), in_specs=[IN_VMEM] * 2...]
  transfers between devices with their start and end apart: 3 -> 3, of which waited for: 2 -> 2; matrix products, arithmetic and copies ran while one was open for 18% -> 19% of each run, Pallas kernels for 8% -> 7%
where the time goes in v3:
time: 68.9 us; the launch traced here: 68.4 us
  waiting for transfers between devices  29.5 us (43%)
  starting transfers between devices  14.4 us (21%)
  Pallas kernels  10.9 us (16%)
  local copies, waits for them, and re-layouts  10.5 us (15%)
  matrix products  2.17 us (3%)
  between operations  0.71 us (1%)
    all_to_all x1, waiting for transfers between devices, fast_shards(): lax.all_to_all(fresh, 'energy', split_axis=0, concat_axis=0, tiled=True)  19.3 us
    all_to_all x1, waiting for transfers between devices, fast_shards(): lax.all_to_all(send, 'energy', split_axis=0, concat_axis=0, tiled=True)  10.2 us
    all_to_all x1, starting transfers between devices, fast_shards(): lax.all_to_all(send, 'energy', split_axis=0, concat_axis=0, tiled=True)  7.87 us
    all_to_all x1, starting transfers between devices, fast_shards(): lax.all_to_all(fresh, 'energy', split_axis=0, concat_axis=0, tiled=True)  5.94 us
    pallas_call x1, Pallas kernels, fast_shards(): pl.pallas_call(near_kernel, out_shape=(pltpu.VMEM((local, slabs, 2, order...  4.78 us
    reshape x1, local copies, waits for them, and re-layouts, fast_shards(): grid_w = screened.reshape(energies, slabs, 2, owned, order)  2.44 us
    pallas_call x1, Pallas kernels, fast_shards(): pl.pallas_call(renew_kernel, out_shape=(out, out), in_specs=[IN_VMEM] * 2...  2.28 us
    dot_general x1, matrix products, fast_shards(): jnp.einsum('pfqe,keqn->kpfn', plain, arranged, precision=lax.Precision.HIGH)  2.17 us
  transfers between devices with their start and end apart: 3, of which 2 were waited for; matrix products, arithmetic and copies ran while one was open for 19% of the time, Pallas kernels for 7%

profile of v3, /device:TPU:0, one launch (start us, length us, event | category | flops | bytes accessed | tf_op | source)
XLA Modules:
  0.0 68.4 jit_solution(9052097379882772869)
XLA Ops:
  0.6 0.6 collective-permute-start
  1.2 4.8 %near.1 = (f32[3,2,2,192,192]{4,3,2,1,0:T(8,128)S(1)}, bf16[3,2,192,192]{3,2,1,0:T(8,128)(2,1)S(1)}) custom-call(bf16[3,2,3,2,192,192]{5,4,3,2,1,0:T(8,128)(2,1)} %green_hbm.1, bf16[3,2,2,192,192]{4,3,2,1,0:T(8,128)(2,1)} %sigma_hbm.1), custom_call_target="tpu_custom_call" | custom-call | tf_op jit(solution)/shard_map/near/pallas_call | solution.py:241
  6.0 0.0 collective-permute-done.halo_ref
  6.0 1.9 %far.1 = bf16[16,3,72,128]{3,2,1,0:T(8,128)(2,1)} custom-call(f32[3,2,2,192,192]{4,3,2,1,0:T(8,128)S(1)} %get-tuple-element.4.total_ref, bf16[3,2,192,192]{3,2,1,0:T(8,128)(2,1)S(1)} %get-tuple-element.5.edge_ref, bf16[3,2,2,192,192]{4,3,2,1,0:T(8,128)(2,1)S(1)} %collective-permute-done.halo_ref), custom_call_target="tpu_custom_call" | custom-call | tf_op jit(solution)/shard_map/far/pallas_call | solution.py:257
  7.9 7.9 %all-to-all-start = ((bf16[16,3,72,128]{3,2,1,0:T(8,128)(2,1)}), bf16[16,3,72,128]{3,2,1,0:T(8,128)(2,1)S(1)}, u32[]{:S(2)}, u32[]{:S(2)}) async-start(bf16[16,3,72,128]{3,2,1,0:T(8,128)(2,1)} %far.1), calls=%async_computation | async-start | bytes 1769472 | tf_op jit(solution)/shard_map/all_to_all | solution.py:266
  15.8 1.8 %copy.12 = f32[48,2,2,2304]{3,0,2,1:T(8,128)S(1)} copy(f32[48,2,2,2304]{3,2,1,0:T(2,128)} %param.8) | data formatting | bytes 3538944 | tf_op args[2]
  17.6 2.4 %reshape.17 = f32[48,2,2,12,192]{4,3,0,2,1:T(8,128)} reshape(f32[48,2,2,2304]{3,0,2,1:T(8,128)S(1)} %copy.12) | data formatting | bytes 3538944 | tf_op jit(solution)/shard_map/reshape | solution.py:269
  20.1 1.5 %slice_bitcast_fusion.1 = (f32[48,2,12,64]{3,2,0,1:T(8,128)S(1)}, f32[48,2,12,64]{3,2,0,1:T(8,128)S(1)}) fusion(f32[48,2,2,12,192]{4,3,0,2,1:T(8,128)} %reshape.17), kind=kLoop, calls=%fused_computation.7 | loop fusion | bytes 1179648 | tf_op jit(solution)/shard_map/squeeze | solution.py:271
  21.5 0.3 pad_maximum_fusion
  21.8 0.1 stack.12
  21.9 1.5 %fusion.6 = (f32[48,1,2,12,128]{4,3,0,2,1:T(8,128)S(1)}, f32[48,1,2,12,128]{4,3,0,2,1:T(8,128)S(1)}) fusion(f32[48,2,2,12,192]{4,3,0,2,1:T(8,128)} %reshape.17), kind=kLoop, calls=%fused_computation.10 | loop fusion | bytes 2359296 | tf_op jit(solution)/shard_map/slice | solution.py:271
  23.4 0.0 copy-start.2
  23.4 0.9 %stack.11 = f32[1,48,2,1536]{3,1,2,0:T(8,128)} reshape(f32[48,1,2,12,128]{4,3,0,2,1:T(8,128)S(1)} %get-tuple-element.7) | data formatting | bytes 1179648 | tf_op jit(solution)/shard_map/stack | solution.py:271
  24.3 0.9 %stack.10 = f32[1,48,2,1536]{3,1,2,0:T(8,128)} reshape(f32[48,1,2,12,128]{4,3,0,2,1:T(8,128)S(1)} %get-tuple-element.6) | data formatting | bytes 1179648 | tf_op jit(solution)/shard_map/stack | solution.py:271
  25.2 0.0 copy-done.2
  25.2 0.0 copy-start
  25.2 0.0 copy-start.1
  25.2 2.2 %fusion = f32[3,1536,2,48,1]{1,3,4,2,0:T(8,128)S(1)} fusion(f32[2,48,2,48,1]{3,1,2,0,4:T(8,128)S(1)} %copy-done.2, f32[1,48,2,1536]{3,1,2,0:T(8,128)S(1)} %stack.12, f32[1,48,2,1536]{3,1,2,0:T(8,128)} %stack.11, f32[1,48,2,1536]{3,1,2,0:T(8,128)} %stack.10), kind=kOutput, calls=%fused_computation.1 | convolution fusion | flops 255688704 | bytes 3575808 | tf_op jit(solution)/shard_map/pfqe,keqn->kpfn/dot_general | solution.py:273
  27.4 10.2 %all-to-all-done.got_ref = bf16[16,3,72,128]{3,2,1,0:T(8,128)(2,1)S(1)} async-done(((bf16[16,3,72,128]{3,2,1,0:T(8,128)(2,1)}), bf16[16,3,72,128]{3,2,1,0:T(8,128)(2,1)S(1)}, u32[]{:S(2)}, u32[]{:S(2)}) %all-to-all-start) | async-done | bytes 884768 | tf_op jit(solution)/shard_map/all_to_all | solution.py:266
  37.6 0.0 copy-done
  37.6 0.0 copy-done.1
  37.6 2.0 %convolve.1 = bf16[16,3,72,128]{3,2,1,0:T(8,128)(2,1)} custom-call(bf16[16,3,72,128]{3,2,1,0:T(8,128)(2,1)S(1)} %all-to-all-done.got_ref, f32[3,96,1536]{2,1,0:T(8,128)S(1)} %bitcast.27, bf16[96,192]{1,0:T(8,128)(2,1)S(1)} %copy-done, bf16[96,192]{1,0:T(8,128)(2,1)S(1)} %copy-done.1), custom_call_target="tpu_custom_call" | custom-call | tf_op jit(solution)/shard_map/convolve/pallas_call | solution.py:276
  39.6 5.9 %all-to-all-start.1 = ((bf16[16,3,72,128]{3,2,1,0:T(8,128)(2,1)}), bf16[16,3,72,128]{3,2,1,0:T(8,128)(2,1)S(1)}, u32[]{:S(2)}, u32[]{:S(2)}) async-start(bf16[16,3,72,128]{3,2,1,0:T(8,128)(2,1)} %convolve.1), calls=%async_computation.1 | async-start | bytes 1769472 | tf_op jit(solution)/shard_map/all_to_all | solution.py:288
  45.5 1.4 %slice.25.green_ref = bf16[3,2,1,2,192,192]{5,4,3,2,1,0:T(8,128)(2,1)S(1)} slice(bf16[3,2,3,2,192,192]{5,4,3,2,1,0:T(8,128)(2,1)} %green_hbm.1), slice={[0:3], [0:2], [1:2], [0:2], [0:192], [0:192]} | slice | bytes 1769472 | tf_op jit(solution)/shard_map/slice | solution.py:304
  46.9 19.3 %all-to-all-done.1.got_ref = bf16[16,3,72,128]{3,2,1,0:T(8,128)(2,1)S(1)} async-done(((bf16[16,3,72,128]{3,2,1,0:T(8,128)(2,1)}), bf16[16,3,72,128]{3,2,1,0:T(8,128)(2,1)S(1)}, u32[]{:S(2)}, u32[]{:S(2)}) %all-to-all-start.1) | async-done | bytes 884768 | tf_op jit(solution)/shard_map/all_to_all | solution.py:288
  66.2 2.3 %renew.1 = (bf16[3,2,2,192,192]{4,3,2,1,0:T(8,128)(2,1)}, bf16[3,2,2,192,192]{4,3,2,1,0:T(8,128)(2,1)}) custom-call(bf16[16,3,72,128]{3,2,1,0:T(8,128)(2,1)S(1)} %all-to-all-done.1.got_ref, bf16[3,2,1,2,192,192]{5,4,3,2,1,0:T(8,128)(2,1)S(1)} %slice.25.green_ref), custom_call_target="tpu_custom_call" | custom-call | tf_op jit(solution)/shard_map/renew/pallas_call | solution.py:291
Async XLA Ops:
  0.6 5.3 %collective-permute-start = (bf16[3,2,2,192,192]{4,3,2,1,0:T(8,128)(2,1)}, bf16[3,2,2,192,192]{4,3,2,1,0:T(8,128)(2,1)S(1)}, u32[]{:S(2)}, u32[]{:S(2)}) collective-permute-start(bf16[3,2,2,192,192]{4,3,2,1,0:T(8,128)(2,1)} %sigma_hbm.1), channel_id=1, source_target_pairs={{0,1},{1,0},{2,3},{3,2},{4,5},{5,4},{6,7},{7,6},{8,9},{9,8},{10,11... | collective-permute-start | bytes 2654216 | tf_op jit(solution)/shard_map/ppermute | solution.py:240
  7.9 29.7 %all-to-all-start = ((bf16[16,3,72,128]{3,2,1,0:T(8,128)(2,1)}), bf16[16,3,72,128]{3,2,1,0:T(8,128)(2,1)S(1)}, u32[]{:S(2)}, u32[]{:S(2)}) async-start(bf16[16,3,72,128]{3,2,1,0:T(8,128)(2,1)} %far.1), calls=%async_computation | async-start | bytes 1769472 | tf_op jit(solution)/shard_map/all_to_all | solution.py:266
  23.4 1.8 %copy-start.2 = (f32[2,48,2,48,1]{3,1,2,0,4:T(8,128)S(1)}, f32[2,48,2,48,1]{3,1,2,0,4:T(8,128)}, u32[]{:S(2)}) copy-start(f32[2,48,2,48,1]{3,1,2,0,4:T(8,128)} %constant.11) | copy-start | bytes 110596
  25.2 12.4 %copy-start = (bf16[96,192]{1,0:T(8,128)(2,1)S(1)}, bf16[96,192]{1,0:T(8,128)(2,1)}, u32[]{:S(2)}) copy-start(bf16[96,192]{1,0:T(8,128)(2,1)} %constant.6.clone.fwd_ref) | copy-start | bytes 110596
  25.2 12.4 %copy-start.1 = (bf16[96,192]{1,0:T(8,128)(2,1)S(1)}, bf16[96,192]{1,0:T(8,128)(2,1)}, u32[]{:S(2)}) copy-start(bf16[96,192]{1,0:T(8,128)(2,1)} %constant.7.clone.bwd_ref) | copy-start | bytes 110596
  39.6 26.6 %all-to-all-start.1 = ((bf16[16,3,72,128]{3,2,1,0:T(8,128)(2,1)}), bf16[16,3,72,128]{3,2,1,0:T(8,128)(2,1)S(1)}, u32[]{:S(2)}, u32[]{:S(2)}) async-start(bf16[16,3,72,128]{3,2,1,0:T(8,128)(2,1)} %convolve.1), calls=%async_computation.1 | async-start | bytes 1769472 | tf_op jit(solution)/shard_map/all_to_all | solution.py:288
